TPU v7x, 32 devices: a whole 2x2x4 slice. The times are simulated.
32 devices in a mesh: pb: 4 (over y, core), ka: 8 (over z, x).
Axes of the slice: x: 2, y: 2, z: 4, core: 2. Of those that a mesh axis runs over, the one named last changes fastest.
Arguments:
- queries: float32 [2048, 128], P('pb'), may hold values from -36 to 36
- cache_keys: float32 [65536, 128], P('ka'), may hold values from -4 to 4
- cache_values: float32 [65536, 128], P('ka'), may hold values from -6 to 6
- kept_index: int32 [4096], P('ka'), may hold values from 0 to 65535, as said below
Outputs:
- fitted: float32 [4096, 128], P('ka')
Inputs may be any that keep to these rules, and one draw needn't show every extreme that they name: `kept_index`: Increasing; the t-th kept index lies among the cache rows t * (16) to (t + 1) * 16 - 1, so the kept keys of a device are rows of its own block of the cache.
All inputs are finite; a program needn't handle non-finite values.
Results may differ from a plain program's by a relative error of at most 0.0003.
Values sent between devices are 32-bit elements; how exact they have to be, the bound alone decides.
A program may use at most 128 MiB of HBM per device.

v0:
```python
import math
import jax
import jax.numpy as jnp
from jax import lax
from jax.sharding import PartitionSpec as P

ITERS = 2
ridge_weight = 0.01
highest = lax.Precision.HIGHEST


def merged_2(part, axis, combine):
    gathered = jax.tree.map(lambda a: lax.all_gather(a, axis), part)

    def take(source):
        return jax.tree.map(lambda a: lax.dynamic_index_in_dim(a, source, 0, False), gathered)

    return lax.fori_loop(
        1, lax.axis_size(axis), lambda source, state: combine(state, take(source)), take(0)
    )


def contract_rows(left_side, right_side):
    return lax.dot_general(
        left_side,
        right_side,
        (((0,), (0,)), ((), ())),
        precision=highest,
        preferred_element_type=jnp.float32,
    )


def contract_cols(left_side, right_side):
    return lax.dot_general(
        left_side,
        right_side,
        (((1,), (1,)), ((), ())),
        precision=highest,
        preferred_element_type=jnp.float32,
    )


def joint_scale(top_one, total_one, top_two, total_two):
    top_joint = jnp.maximum(top_one, top_two)
    factor_one = jnp.exp(top_one - top_joint)
    factor_two = jnp.exp(top_two - top_joint)
    return (top_joint, total_one * factor_one + total_two * factor_two, factor_one, factor_two)


def combine_target(part_one, part_two):
    top_joint, total_sum, factor_one, factor_two = joint_scale(
        part_one[0], part_one[1], part_two[0], part_two[1]
    )
    numerator = part_one[2] * factor_one[:, None] + part_two[2] * factor_two[:, None]
    return (top_joint, total_sum, numerator)


def combine_stats(part_one, part_two):
    target_part = combine_target(part_one[0:3], part_two[0:3])
    kept_top, kept_total, factor_one, factor_two = joint_scale(
        part_one[3], part_one[4], part_two[3], part_two[4]
    )
    return target_part + (kept_top, kept_total)


def key_rows(weights, updates):
    return lax.psum(contract_rows(weights, updates), "pb")


def forward_terms(weights, direction):
    return (
        jnp.dot(weights, direction, precision=highest, preferred_element_type=jnp.float32),
        jnp.sum(direction * direction, axis=0),
    )


def residual_total(column_part):
    return lax.psum(column_part, "ka")


def direction_total(column_part):
    return lax.psum(column_part, "ka")


def shards(queries, cache_keys, cache_values, kept_index):
    head_width = queries.shape[1]
    inverse_root = 1.0 / math.sqrt(head_width)
    cache_rows = cache_keys.shape[0]
    block_size = min(1024, cache_rows)
    target_stats = None
    for block_number in range(cache_rows // block_size):
        keys_block = lax.slice_in_dim(
            cache_keys, block_number * block_size, (block_number + 1) * block_size, axis=0
        )
        values_block = lax.slice_in_dim(
            cache_values, block_number * block_size, (block_number + 1) * block_size, axis=0
        )
        scores = contract_cols(queries, keys_block) * inverse_root
        top_block = jnp.max(scores, axis=1)
        exponent_block = jnp.exp(scores - top_block[:, None])
        stats_block = (
            top_block,
            jnp.sum(exponent_block, axis=1),
            jnp.dot(
                exponent_block, values_block, precision=highest, preferred_element_type=jnp.float32
            ),
        )
        target_stats = (
            stats_block if target_stats is None else combine_target(target_stats, stats_block)
        )
    local_kept = kept_index - lax.axis_index("ka") * cache_rows
    kept_keys = jnp.take(cache_keys, local_kept, axis=0)
    kept_scores = contract_cols(queries, kept_keys) * inverse_root
    kept_top = jnp.max(kept_scores, axis=1)
    kept_exponent = jnp.exp(kept_scores - kept_top[:, None])
    merged = merged_2(
        (
            target_stats[0],
            target_stats[1],
            target_stats[2],
            kept_top,
            jnp.sum(kept_exponent, axis=1),
        ),
        "ka",
        combine_stats,
    )
    target = merged[2] / merged[1][:, None]
    weights = kept_exponent * (jnp.exp(kept_top - merged[3]) / merged[4])[:, None]
    residual = key_rows(weights, target)
    fitted = jnp.zeros_like(residual)
    direction = residual
    norm_now = residual_total(jnp.sum(residual * residual, axis=0))
    for iteration in range(ITERS):
        final_turn = iteration + 1 == ITERS
        update_part, square_part = forward_terms(weights, direction)
        updates = lax.psum(update_part, "ka")
        operator_image = key_rows(weights, updates) + ridge_weight * direction
        step_length = norm_now / direction_total(jnp.sum(direction * operator_image, axis=0))
        fitted = fitted + step_length * direction
        if not final_turn:
            residual = residual - step_length * operator_image
            norm_next = residual_total(jnp.sum(residual * residual, axis=0))
            direction = residual + norm_next / norm_now * direction
            norm_now = norm_next
    return fitted


def solution(mesh):
    in_specs = (P("pb", None), P("ka", None), P("ka", None), P("ka"))
    out_specs = P("ka", None)
    return jax.shard_map(shards, mesh=mesh, in_specs=in_specs, out_specs=out_specs, check_vma=False)
```

profile of v0, /device:TPU:0, one launch (start us, length us, event | category | flops | bytes accessed | tf_op | source)
XLA Modules:
  0.0 488.6 jit_solution(1318856065512095628)
XLA Ops:
  7.5 3.1 multiply_reduce_fusion
  10.6 3.0 multiply_reduce_fusion.1
  17.6 2.0 multiply_reduce_fusion.4
  19.6 2.0 multiply_reduce_fusion.5
  21.6 2.4 multiply_reduce_fusion.6
  24.0 2.0 multiply_reduce_fusion.7
  26.1 2.0 fusion.18
  28.1 2.0 fusion.19
  30.1 2.0 fusion.20
  32.1 2.0 fusion.21
  34.1 2.2 fusion.22
  36.3 2.0 fusion.23
  38.4 2.1 fusion.36
  40.5 2.7 fusion.37
  50.7 28.0 %all-gather.3 = f32[8,1,512]{2,1,0:T(1,128)S(1)} all-gather(f32[1,1,512]{2,1,0:T(1,128)S(1)} %get-tuple-element.319), channel_id=1, replica_groups=mesh['pb'=4,'ka'=8] {'ka'}, dimensions={0}, use_global_device_ids=true | all-gather | bytes 18432 | tf_op jit(solution)/shard_map/all_gather | solution.py:13
  78.7 26.2 %all-gather.4 = f32[8,1,512]{2,1,0:T(1,128)S(1)} all-gather(f32[1,1,512]{2,1,0:T(1,128)S(1)} %get-tuple-element.318), channel_id=1, replica_groups=mesh['pb'=4,'ka'=8] {'ka'}, dimensions={0}, use_global_device_ids=true | all-gather | bytes 18432 | tf_op jit(solution)/shard_map/all_gather | solution.py:13
  105.0 3.2 gather_fusion
  109.2 26.0 %all-gather.5 = f32[8,1,512]{2,1,0:T(1,128)S(1)} all-gather(f32[1,1,512]{2,1,0:T(1,128)S(1)} %bitcast.74), channel_id=3, replica_groups=mesh['pb'=4,'ka'=8] {'ka'}, dimensions={0}, use_global_device_ids=true | all-gather | bytes 18432 | tf_op jit(solution)/shard_map/all_gather | solution.py:13
  135.5 26.0 %all-gather.6 = f32[8,1,512]{2,1,0:T(1,128)S(1)} all-gather(f32[1,1,512]{2,1,0:T(1,128)S(1)} %bitcast.91), channel_id=4, replica_groups=mesh['pb'=4,'ka'=8] {'ka'}, dimensions={0}, use_global_device_ids=true | all-gather | bytes 18432 | tf_op jit(solution)/shard_map/all_gather | solution.py:13
  162.4 9.3 %while.23 = (s32[]{:T(128)}, f32[512]{0:T(512)S(1)}, f32[512]{0:T(512)S(1)}, f32[512,128]{1,0:T(8,128)S(1)}, f32[512]{0:T(512)S(1)}, /*index=5*/f32[512]{0:T(512...) while((s32[]{:T(128)}, f32[512]{0:T(512)S(1)}, ...), condition=%wide.region_19.20_spmd, body=%wide.region_18.19_spmd.sunk | while | flops 202757 | bytes 835779 | solution.py:18
  173.6 29.4 %all-reduce.7.cloned.1.call-done = f32[512,128]{1,0:T(8,128)} async-done(((f32[512,128]{1,0:T(8,128)}), f32[512,128]{1,0:T(8,128)}) %all-reduce.7.cloned.1.call-update) | async-done | bytes 262160 | tf_op jit(solution)/shard_map/psum | solution.py:67
  203.0 3.5 fusion.86
  206.6 70.7 %all-reduce.9.cloned.1.call-done = f32[512,128]{1,0:T(8,128)} async-done(((f32[512,128]{1,0:T(8,128)}), f32[512,128]{1,0:T(8,128)}) %all-reduce.9.cloned.1.call-update) | async-done | bytes 262160 | tf_op jit(solution)/shard_map/psum | solution.py:136
  277.2 2.7 fusion.84
  280.0 31.4 %all-reduce.11.cloned.1.call-done = f32[512,128]{1,0:T(8,128)} async-done(((f32[512,128]{1,0:T(8,128)}), f32[512,128]{1,0:T(8,128)}) %all-reduce.11.cloned.1.call-update) | async-done | bytes 262160 | tf_op jit(solution)/shard_map/psum | solution.py:67
  312.4 21.3 %all-reduce = (f32[128]{0:T(128)S(1)}, f32[128]{0:T(128)S(1)}) all-reduce(f32[128]{0:T(128)S(1)} %get-tuple-element.277, f32[128]{0:T(128)S(1)} %get-tuple-element.276), channel_id=1, replica_groups=mesh['pb'=4,'ka'=8] {'ka'}, use_global_device_ids=true, to_apply=%region_22.23 | all-reduce | flops 256 | bytes 2048 | tf_op jit(solution)/shard_map/psum | solution.py:78
  334.8 17.3 %psum.68 = f32[128]{0:T(128)S(1)} all-reduce(f32[128]{0:T(128)S(1)} %multiply_reduce_fusion.9), channel_id=1, replica_groups=mesh['pb'=4,'ka'=8] {'ka'}, use_global_device_ids=true, to_apply=%region_28.29 | all-reduce | flops 128 | bytes 1024 | tf_op jit(solution)/shard_map/psum | solution.py:78
  352.1 3.5 fusion.82
  355.7 68.5 %all-reduce.13.cloned.1.call-done = f32[512,128]{1,0:T(8,128)} async-done(((f32[512,128]{1,0:T(8,128)}), f32[512,128]{1,0:T(8,128)}) %all-reduce.13.cloned.1.call-update) | async-done | bytes 262160 | tf_op jit(solution)/shard_map/psum | solution.py:136
  424.1 2.7 fusion.80
  426.9 31.4 %all-reduce.15.cloned.1.call-done = f32[512,128]{1,0:T(8,128)} async-done(((f32[512,128]{1,0:T(8,128)}), f32[512,128]{1,0:T(8,128)}) %all-reduce.15.cloned.1.call-update) | async-done | bytes 262160 | tf_op jit(solution)/shard_map/psum | solution.py:67
  459.3 21.3 %psum.71 = f32[128]{0:T(128)S(1)} all-reduce(f32[128]{0:T(128)S(1)} %multiply_reduce_fusion.8), channel_id=1, replica_groups=mesh['pb'=4,'ka'=8] {'ka'}, use_global_device_ids=true, to_apply=%region_32.33 | all-reduce | flops 128 | bytes 1024 | tf_op jit(solution)/shard_map/psum | solution.py:82
  (130 shorter events, 29.6 us)
Async XLA Ops:
  6.5 1.0 copy-start
  6.5 154.9 %all-gather.9.cloned.1.call-start = ((), (), s32[]{:S(2)}) async-start(), calls=%async_computation.5 | async-start | bytes 2359296 | tf_op jit(solution)/shard_map/all_gather | solution.py:13
  7.5 6.2 %copy-start.15 = (f32[8192,128]{1,0:T(8,128)S(1)}, f32[8192,128]{1,0:T(8,128)}, u32[]{:S(2)}) copy-start(f32[8192,128]{1,0:T(8,128)} %param.7) | copy-start | bytes 12582916
  13.7 12.4 %copy-start.1 = (f32[512,1024]{1,0:T(8,128)}, f32[512,1024]{1,0:T(8,128)S(1)}, u32[]{:S(2)}) copy-start(f32[512,1024]{1,0:T(8,128)S(1)} %get-tuple-element.346) | copy-start | bytes 6291460
  15.6 12.4 %copy-start.3 = (f32[512,1024]{1,0:T(8,128)}, f32[512,1024]{1,0:T(8,128)S(1)}, u32[]{:S(2)}) copy-start(f32[512,1024]{1,0:T(8,128)S(1)} %get-tuple-element.348) | copy-start | bytes 6291460
  17.6 12.5 %copy-start.5 = (f32[512,1024]{1,0:T(8,128)}, f32[512,1024]{1,0:T(8,128)S(1)}, u32[]{:S(2)}) copy-start(f32[512,1024]{1,0:T(8,128)S(1)} %get-tuple-element.350) | copy-start | bytes 6291460
  19.6 12.5 %copy-start.7 = (f32[512,1024]{1,0:T(8,128)}, f32[512,1024]{1,0:T(8,128)S(1)}, u32[]{:S(2)}) copy-start(f32[512,1024]{1,0:T(8,128)S(1)} %get-tuple-element.352) | copy-start | bytes 6291460
  21.6 12.6 %copy-start.9 = (f32[512,1024]{1,0:T(8,128)}, f32[512,1024]{1,0:T(8,128)S(1)}, u32[]{:S(2)}) copy-start(f32[512,1024]{1,0:T(8,128)S(1)} %get-tuple-element.354) | copy-start | bytes 6291460
  21.6 4.5 copy-start.18
  24.0 12.3 %copy-start.11 = (f32[512,1024]{1,0:T(8,128)}, f32[512,1024]{1,0:T(8,128)S(1)}, u32[]{:S(2)}) copy-start(f32[512,1024]{1,0:T(8,128)S(1)} %get-tuple-element.356) | copy-start | bytes 6291460
  26.0 12.4 %copy-start.13 = (f32[512,1024]{1,0:T(8,128)}, f32[512,1024]{1,0:T(8,128)S(1)}, u32[]{:S(2)}) copy-start(f32[512,1024]{1,0:T(8,128)S(1)} %get-tuple-element.358) | copy-start | bytes 6291460
  43.2 159.8 %all-reduce.7.cloned.1.call-start = ((), (), s32[]{:S(2)}) async-start(), calls=%async_computation | async-start | bytes 524288 | tf_op jit(solution)/shard_map/psum | solution.py:67
  43.3 1.6 copy-start.2
  43.3 2.2 copy-start.4
  44.9 1.7 copy-start.6
  45.5 1.7 copy-start.8
  46.6 1.7 copy-start.10
  47.2 1.7 copy-start.12
  48.3 1.7 copy-start.14
  48.9 56.0 %copy-start.19 = (s32[512]{0:T(512)S(1)}, s32[512]{0:T(512)}, u32[]{:S(2)}) copy-start(s32[512]{0:T(512)} %param.9) | copy-start | bytes 6148
  173.6 103.7 %all-reduce.9.cloned.1.call-start = ((), (), s32[]{:S(2)}) async-start(), calls=%async_computation.1 | async-start | bytes 524288 | tf_op jit(solution)/shard_map/psum | solution.py:136
  203.0 108.4 %copy-start.16 = (f32[512,128]{1,0:T(8,128)S(1)}, f32[512,128]{1,0:T(8,128)}, u32[]{:S(2)}) copy-start(f32[512,128]{1,0:T(8,128)} %all-reduce.7.cloned.1.call-done) | copy-start | bytes 786436
  206.5 104.8 %all-reduce.11.cloned.1.call-start = ((), (), s32[]{:S(2)}) async-start(), calls=%async_computation.2 | async-start | bytes 524288 | tf_op jit(solution)/shard_map/psum | solution.py:67
  280.0 144.2 %all-reduce.13.cloned.1.call-start = ((), (), s32[]{:S(2)}) async-start(), calls=%async_computation.3 | async-start | bytes 524288 | tf_op jit(solution)/shard_map/psum | solution.py:136
  334.8 123.5 %copy-start.17 = (f32[512,128]{1,0:T(8,128)S(1)}, f32[512,128]{1,0:T(8,128)}, u32[]{:S(2)}) copy-start(f32[512,128]{1,0:T(8,128)} %all-reduce.11.cloned.1.call-done) | copy-start | bytes 786436
  355.6 102.6 %all-reduce.15.cloned.1.call-start = ((), (), s32[]{:S(2)}) async-start(), calls=%async_computation.4 | async-start | bytes 524288 | tf_op jit(solution)/shard_map/psum | solution.py:67
Sparse Core Ops, SparseCore 0:
  43.3 52.1 all-gather.8
  173.7 29.2 all-reduce.6
  206.7 70.5 all-reduce.8
  280.1 31.2 all-reduce.10
  355.8 68.3 all-reduce.12
  427.0 31.2 all-reduce.14
where the time goes:
time: 498 us; the launch traced here: 489 us
  waiting for transfers between devices  231 us (46%)
  blocking collectives  166 us (33%)
  matrix products  50.8 us (10%)
  other arithmetic  17.1 us (3%)
  between operations  14 us (3%)
  local copies, waits for them, and re-layouts  8.61 us (2%)
    psum x2, waiting for transfers between devices, shards(): updates = lax.psum(update_part, 'ka')  139 us
    all_gather x4, blocking collectives, merged_2(): gathered = jax.tree.map(lambda a: lax.all_gather(a, axis), part)  106 us
    psum x3, waiting for transfers between devices, key_rows(): return lax.psum(contract_rows(weights, updates), 'pb')  92.1 us
    psum x2, blocking collectives, residual_total(): return lax.psum(column_part, 'ka')  38.6 us
    psum x1, blocking collectives, direction_total(): return lax.psum(column_part, 'ka')  21.3 us
    dot_general x9, matrix products, contract_cols(): lax.dot_general(left_side, right_side, (((1,), (1,)), ((), ())), precisio...  19.5 us
    dot_general x8, matrix products, shards(): jnp.dot(exponent_block, values_block, precision=highest, preferred_elemen...  17 us
  transfers between devices with their start and end apart: 6, of which 5 were waited for; matrix products, arithmetic and copies ran while one was open for 2% of the time, Pallas kernels for 0%

commit v1 on v0

--- a/solution.py
+++ b/solution.py
@@ -7,6 +7,10 @@
 ITERS = 2
 ridge_weight = 0.01
 highest = lax.Precision.HIGHEST
+
+
+def vectors_change(vector):
+    return jnp.sum(lax.all_gather(vector, "ka"), 0)
 
 
 def merged_2(part, axis, combine):
@@ -75,7 +79,7 @@
 
 
 def residual_total(column_part):
-    return lax.psum(column_part, "ka")
+    return vectors_change(column_part)
 
 
 def direction_total(column_part):

time: 498 us -> 514 us (1.032)
  blocking collectives: 166 us -> 183 us
    all_gather x0 -> x2, blocking collectives: none -> 38.7 us  [vectors_change(): return jnp.sum(lax.all_gather(vector, 'ka'), 0)]
    psum x2 -> x0, blocking collectives: 38.6 us -> none  [residual_total(): return lax.psum(column_part, 'ka')]
    psum x1 -> x2, blocking collectives: 21.3 us -> 38.5 us  [direction_total(): return lax.psum(column_part, 'ka')]
where the time goes in v1:
time: 514 us; the launch traced here: 504 us
  waiting for transfers between devices  230 us (45%)
  blocking collectives  183 us (36%)
  matrix products  50.8 us (10%)
  other arithmetic  17.1 us (3%)
  between operations  14 us (3%)
  local copies, waits for them, and re-layouts  8.61 us (2%)
    psum x2, waiting for transfers between devices, shards(): updates = lax.psum(update_part, 'ka')  138 us
    all_gather x4, blocking collectives, merged_2(): gathered = jax.tree.map(lambda a: lax.all_gather(a, axis), part)  106 us
    psum x3, waiting for transfers between devices, key_rows(): return lax.psum(contract_rows(weights, updates), 'pb')  92.1 us
    all_gather x2, blocking collectives, vectors_change(): return jnp.sum(lax.all_gather(vector, 'ka'), 0)  38.7 us
    psum x2, blocking collectives, direction_total(): return lax.psum(column_part, 'ka')  38.5 us
    dot_general x9, matrix products, contract_cols(): lax.dot_general(left_side, right_side, (((1,), (1,)), ((), ())), precisio...  19.5 us
    dot_general x8, matrix products, shards(): jnp.dot(exponent_block, values_block, precision=highest, preferred_elemen...  17 us
  transfers between devices with their start and end apart: 6, of which 5 were waited for; matrix products, arithmetic and copies ran while one was open for 2% of the time, Pallas kernels for 0%

profile of v1, /device:TPU:0, one launch (start us, length us, event | category | flops | bytes accessed | tf_op | source)
XLA Modules:
  0.0 504.2 jit_solution(15698568379458818211)
XLA Ops:
  7.5 3.1 multiply_reduce_fusion
  10.6 3.0 multiply_reduce_fusion.1
  17.6 2.0 multiply_reduce_fusion.4
  19.6 2.0 multiply_reduce_fusion.5
  21.6 2.4 multiply_reduce_fusion.6
  26.1 2.0 fusion.18
  28.1 2.0 fusion.19
  30.1 2.0 fusion.20
  32.1 2.0 fusion.21
  34.1 2.2 fusion.22
  36.3 2.0 fusion.23
  38.4 2.1 fusion.36
  40.5 2.7 fusion.37
  50.7 28.0 %all-gather.5 = f32[8,1,512]{2,1,0:T(1,128)S(1)} all-gather(f32[1,1,512]{2,1,0:T(1,128)S(1)} %get-tuple-element.317), channel_id=1, replica_groups=mesh['pb'=4,'ka'=8] {'ka'}, dimensions={0}, use_global_device_ids=true | all-gather | bytes 18432 | tf_op jit(solution)/shard_map/all_gather | solution.py:17
  78.7 26.2 %all-gather.6 = f32[8,1,512]{2,1,0:T(1,128)S(1)} all-gather(f32[1,1,512]{2,1,0:T(1,128)S(1)} %get-tuple-element.316), channel_id=1, replica_groups=mesh['pb'=4,'ka'=8] {'ka'}, dimensions={0}, use_global_device_ids=true | all-gather | bytes 18432 | tf_op jit(solution)/shard_map/all_gather | solution.py:17
  105.0 3.2 gather_fusion
  109.2 26.0 %all-gather.7 = f32[8,1,512]{2,1,0:T(1,128)S(1)} all-gather(f32[1,1,512]{2,1,0:T(1,128)S(1)} %bitcast.76), channel_id=3, replica_groups=mesh['pb'=4,'ka'=8] {'ka'}, dimensions={0}, use_global_device_ids=true | all-gather | bytes 18432 | tf_op jit(solution)/shard_map/all_gather | solution.py:17
  135.5 26.0 %all-gather.8 = f32[8,1,512]{2,1,0:T(1,128)S(1)} all-gather(f32[1,1,512]{2,1,0:T(1,128)S(1)} %bitcast.93), channel_id=4, replica_groups=mesh['pb'=4,'ka'=8] {'ka'}, dimensions={0}, use_global_device_ids=true | all-gather | bytes 18432 | tf_op jit(solution)/shard_map/all_gather | solution.py:17
  162.4 9.3 %while.23 = (s32[]{:T(128)}, f32[512]{0:T(512)S(1)}, f32[512]{0:T(512)S(1)}, f32[512,128]{1,0:T(8,128)S(1)}, f32[512]{0:T(512)S(1)}, /*index=5*/f32[512]{0:T(512...) while((s32[]{:T(128)}, f32[512]{0:T(512)S(1)}, ...), condition=%wide.region_19.20_spmd, body=%wide.region_18.19_spmd.sunk | while | flops 202757 | bytes 835779 | solution.py:22
  173.6 29.4 %all-reduce.6.cloned.1.call-done = f32[512,128]{1,0:T(8,128)} async-done(((f32[512,128]{1,0:T(8,128)}), f32[512,128]{1,0:T(8,128)}) %all-reduce.6.cloned.1.call-update) | async-done | bytes 262160 | tf_op jit(solution)/shard_map/psum | solution.py:71
  203.0 3.5 fusion.86
  206.6 70.7 %all-reduce.8.cloned.1.call-done = f32[512,128]{1,0:T(8,128)} async-done(((f32[512,128]{1,0:T(8,128)}), f32[512,128]{1,0:T(8,128)}) %all-reduce.8.cloned.1.call-update) | async-done | bytes 262160 | tf_op jit(solution)/shard_map/psum | solution.py:140
  277.2 2.7 fusion.84
  280.0 31.4 %all-reduce.10.cloned.1.call-done = f32[512,128]{1,0:T(8,128)} async-done(((f32[512,128]{1,0:T(8,128)}), f32[512,128]{1,0:T(8,128)}) %all-reduce.10.cloned.1.call-update) | async-done | bytes 262160 | tf_op jit(solution)/shard_map/psum | solution.py:71
  312.4 20.4 %all-gather.9 = f32[8,1,128]{2,1,0:T(1,128)S(1)} all-gather(f32[1,1,128]{2,1,0:T(1,128)S(1)} %bitcast.102), channel_id=5, replica_groups=mesh['pb'=4,'ka'=8] {'ka'}, dimensions={0}, use_global_device_ids=true | all-gather | bytes 4608 | tf_op jit(solution)/shard_map/all_gather | solution.py:13
  332.8 17.1 %psum.52 = f32[128]{0:T(128)S(1)} all-reduce(f32[128]{0:T(128)S(1)} %get-tuple-element.276), channel_id=1, replica_groups=mesh['pb'=4,'ka'=8] {'ka'}, use_global_device_ids=true, to_apply=%region_26.27 | all-reduce | flops 128 | bytes 1024 | tf_op jit(solution)/shard_map/psum | solution.py:86
  351.0 18.3 %all-gather.10 = f32[8,1,128]{2,1,0:T(1,128)S(1)} all-gather(f32[1,1,128]{2,1,0:T(1,128)S(1)} %bitcast.103), channel_id=6, replica_groups=mesh['pb'=4,'ka'=8] {'ka'}, dimensions={0}, use_global_device_ids=true | all-gather | bytes 4608 | tf_op jit(solution)/shard_map/all_gather | solution.py:13
  369.3 3.5 fusion.82
  372.9 66.9 %all-reduce.12.cloned.1.call-done = f32[512,128]{1,0:T(8,128)} async-done(((f32[512,128]{1,0:T(8,128)}), f32[512,128]{1,0:T(8,128)}) %all-reduce.12.cloned.1.call-update) | async-done | bytes 262160 | tf_op jit(solution)/shard_map/psum | solution.py:140
  439.8 2.7 fusion.80
  442.5 31.4 %all-reduce.14.cloned.1.call-done = f32[512,128]{1,0:T(8,128)} async-done(((f32[512,128]{1,0:T(8,128)}), f32[512,128]{1,0:T(8,128)}) %all-reduce.14.cloned.1.call-update) | async-done | bytes 262160 | tf_op jit(solution)/shard_map/psum | solution.py:71
  475.0 21.3 %psum.55 = f32[128]{0:T(128)S(1)} all-reduce(f32[128]{0:T(128)S(1)} %multiply_reduce_fusion.8), channel_id=1, replica_groups=mesh['pb'=4,'ka'=8] {'ka'}, use_global_device_ids=true, to_apply=%region_32.33 | all-reduce | flops 128 | bytes 1024 | tf_op jit(solution)/shard_map/psum | solution.py:86
  (133 shorter events, 31.6 us)
Async XLA Ops:
  6.5 1.0 copy-start
  6.5 154.9 %all-gather.13.cloned.1.call-start = ((), (), s32[]{:S(2)}) async-start(), calls=%async_computation.5 | async-start | bytes 2359296 | tf_op jit(solution)/shard_map/all_gather | solution.py:17
  7.5 6.2 %copy-start.15 = (f32[8192,128]{1,0:T(8,128)S(1)}, f32[8192,128]{1,0:T(8,128)}, u32[]{:S(2)}) copy-start(f32[8192,128]{1,0:T(8,128)} %param.7) | copy-start | bytes 12582916
  13.7 12.4 %copy-start.1 = (f32[512,1024]{1,0:T(8,128)}, f32[512,1024]{1,0:T(8,128)S(1)}, u32[]{:S(2)}) copy-start(f32[512,1024]{1,0:T(8,128)S(1)} %get-tuple-element.344) | copy-start | bytes 6291460
  15.6 12.4 %copy-start.3 = (f32[512,1024]{1,0:T(8,128)}, f32[512,1024]{1,0:T(8,128)S(1)}, u32[]{:S(2)}) copy-start(f32[512,1024]{1,0:T(8,128)S(1)} %get-tuple-element.346) | copy-start | bytes 6291460
  17.6 12.5 %copy-start.5 = (f32[512,1024]{1,0:T(8,128)}, f32[512,1024]{1,0:T(8,128)S(1)}, u32[]{:S(2)}) copy-start(f32[512,1024]{1,0:T(8,128)S(1)} %get-tuple-element.348) | copy-start | bytes 6291460
  19.6 12.5 %copy-start.7 = (f32[512,1024]{1,0:T(8,128)}, f32[512,1024]{1,0:T(8,128)S(1)}, u32[]{:S(2)}) copy-start(f32[512,1024]{1,0:T(8,128)S(1)} %get-tuple-element.350) | copy-start | bytes 6291460
  21.6 12.6 %copy-start.9 = (f32[512,1024]{1,0:T(8,128)}, f32[512,1024]{1,0:T(8,128)S(1)}, u32[]{:S(2)}) copy-start(f32[512,1024]{1,0:T(8,128)S(1)} %get-tuple-element.352) | copy-start | bytes 6291460
  21.6 4.5 copy-start.18
  24.0 12.3 %copy-start.11 = (f32[512,1024]{1,0:T(8,128)}, f32[512,1024]{1,0:T(8,128)S(1)}, u32[]{:S(2)}) copy-start(f32[512,1024]{1,0:T(8,128)S(1)} %get-tuple-element.354) | copy-start | bytes 6291460
  26.0 12.4 %copy-start.13 = (f32[512,1024]{1,0:T(8,128)}, f32[512,1024]{1,0:T(8,128)S(1)}, u32[]{:S(2)}) copy-start(f32[512,1024]{1,0:T(8,128)S(1)} %get-tuple-element.356) | copy-start | bytes 6291460
  43.2 159.8 %all-reduce.6.cloned.1.call-start = ((), (), s32[]{:S(2)}) async-start(), calls=%async_computation | async-start | bytes 524288 | tf_op jit(solution)/shard_map/psum | solution.py:71
  43.3 1.6 copy-start.2
  43.3 2.2 copy-start.4
  44.9 1.7 copy-start.6
  45.5 1.7 copy-start.8
  46.6 1.7 copy-start.10
  47.2 1.7 copy-start.12
  48.3 1.7 copy-start.14
  48.9 56.0 %copy-start.19 = (s32[512]{0:T(512)S(1)}, s32[512]{0:T(512)}, u32[]{:S(2)}) copy-start(s32[512]{0:T(512)} %param.9) | copy-start | bytes 6148
  173.6 103.7 %all-reduce.8.cloned.1.call-start = ((), (), s32[]{:S(2)}) async-start(), calls=%async_computation.1 | async-start | bytes 524288 | tf_op jit(solution)/shard_map/psum | solution.py:140
  203.0 108.4 %copy-start.16 = (f32[512,128]{1,0:T(8,128)S(1)}, f32[512,128]{1,0:T(8,128)}, u32[]{:S(2)}) copy-start(f32[512,128]{1,0:T(8,128)} %all-reduce.6.cloned.1.call-done) | copy-start | bytes 786436
  206.5 104.8 %all-reduce.10.cloned.1.call-start = ((), (), s32[]{:S(2)}) async-start(), calls=%async_computation.2 | async-start | bytes 524288 | tf_op jit(solution)/shard_map/psum | solution.py:71
  280.0 159.8 %all-reduce.12.cloned.1.call-start = ((), (), s32[]{:S(2)}) async-start(), calls=%async_computation.3 | async-start | bytes 524288 | tf_op jit(solution)/shard_map/psum | solution.py:140
  351.0 123.0 %copy-start.17 = (f32[512,128]{1,0:T(8,128)S(1)}, f32[512,128]{1,0:T(8,128)}, u32[]{:S(2)}) copy-start(f32[512,128]{1,0:T(8,128)} %all-reduce.10.cloned.1.call-done) | copy-start | bytes 786436
  372.9 101.1 %all-reduce.14.cloned.1.call-start = ((), (), s32[]{:S(2)}) async-start(), calls=%async_computation.4 | async-start | bytes 524288 | tf_op jit(solution)/shard_map/psum | solution.py:71
Sparse Core Ops, SparseCore 0:
  43.3 52.1 all-gather.12
  173.7 29.2 all-reduce.5
  206.7 70.5 all-reduce.7
  280.1 31.2 all-reduce.9
  373.0 66.7 all-reduce.11
  442.6 31.2 all-reduce.13
